TPU v7x, 32 devices: a whole 2x2x4 slice. The times are simulated.
32 devices in a mesh: grp: 2 (over y), dev: 16 (over z, x, core).
Axes of the slice: x: 2, y: 2, z: 4, core: 2. Of those that a mesh axis runs over, the one named last changes fastest.
Arguments:
- spectra: float32 [256, 2, 2, 4096], P(('grp', 'dev')), may hold values from -100 to 100
- source_pick: int32 [32], P(('grp', 'dev')), may hold values from 0 to 7
- pair_remote: int32 [2, 16, 2, 2], P('grp', 'dev'), may hold values from 0 to 7
- pair_local: int32 [2, 16, 2, 2], P('grp', 'dev'), may hold values from 0 to 7
- pair_count: int32 [2, 16, 2], P('grp', 'dev'), may hold values from 0 to 2, as said below
Outputs:
- group_corr: float32 [256, 16, 512], P(('grp', 'dev'))
- cross_corr: float32 [2, 16, 2, 2, 512], P('grp', 'dev')
Inputs may be any that keep to these rules, and one draw needn't show every extreme that they name: `pair_count`: A block has no pairs with its own group and at most 2 with any other; in every group some block has exactly 2 with some other group.
All inputs are finite; a program needn't handle non-finite values.
Results may differ from a plain program's by a relative error of at most 0.0075.
Values may be sent and summed in bfloat16 or wider, within the bound.
A program may use at most 64 MiB of HBM per device.

v0:
```python
import math

import jax
import jax.numpy as jnp
from jax import lax
from jax.sharding import PartitionSpec as P

F = 4096
LAGS = 512
LAG_BLK = 128
BAND = 64


source_block = 16


def whiten(spectra):
    magnitude = jnp.sqrt(spectra[:, :, 0] * spectra[:, :, 0] + spectra[:, :, 1] * spectra[:, :, 1])
    rows_here, segments, bins = magnitude.shape
    band_mean = jnp.mean(magnitude.reshape(rows_here, segments, bins // BAND, BAND), axis=3) + 1e-05
    divisor = jnp.repeat(band_mean, BAND, axis=2)
    return (spectra / divisor[:, :, None, :]).astype(jnp.bfloat16)


def lag_tables():
    frequency = jnp.arange(F, dtype=jnp.int32)
    lag_index = jnp.arange(LAG_BLK, dtype=jnp.int32)
    phase_index = frequency[:, None] * lag_index[None, :] % (2 * F)
    angles = phase_index.astype(jnp.float32) * (math.pi / F)
    return (jnp.cos(angles).astype(jnp.bfloat16), (-jnp.sin(angles)).astype(jnp.bfloat16))


def lag_turn(block_index):
    frequency = jnp.arange(F, dtype=jnp.int32)
    phase_index = frequency * (LAG_BLK * block_index - LAGS // 2) % (2 * F)
    angles = phase_index.astype(jnp.float32) * (math.pi / F)
    return (jnp.cos(angles), jnp.sin(angles))


def cross_to_lags(cross_real, cross_imag, tables):
    cos_table, sin_table = tables
    lag_blocks = []
    for block_index in range(LAGS // LAG_BLK):
        turn_cos, turn_sin = lag_turn(block_index)
        rot_real = (cross_real * turn_cos - cross_imag * turn_sin).astype(jnp.bfloat16)
        rot_imag = (cross_real * turn_sin + cross_imag * turn_cos).astype(jnp.bfloat16)
        lag_blocks.append(
            jnp.dot(rot_real, cos_table, preferred_element_type=jnp.float32)
            + jnp.dot(rot_imag, sin_table, preferred_element_type=jnp.float32)
        )
    return jnp.concatenate(lag_blocks, axis=1) * F ** (-0.5)


def outer_cross(left_rows, right_rows):
    left_float = left_rows.astype(jnp.float32)
    right_float = right_rows.astype(jnp.float32)
    segments = left_rows.shape[1]
    cross_real = jnp.zeros((left_rows.shape[0], right_rows.shape[0], F), jnp.float32)
    cross_imag = jnp.zeros((left_rows.shape[0], right_rows.shape[0], F), jnp.float32)
    for segment in range(segments):
        left_real = left_float[:, segment, 0][:, None]
        left_imag = left_float[:, segment, 1][:, None]
        right_real = right_float[:, segment, 0][None]
        right_imag = right_float[:, segment, 1][None]
        cross_real = cross_real + (left_real * right_real + left_imag * right_imag)
        cross_imag = cross_imag + (left_imag * right_real - left_real * right_imag)
    inverse = 1.0 / segments
    return ((cross_real * inverse).reshape(-1, F), (cross_imag * inverse).reshape(-1, F))


def pair_cross(left_rows, right_rows):
    left_float = left_rows.astype(jnp.float32)
    right_float = right_rows.astype(jnp.float32)
    segments = left_rows.shape[1]
    cross_real = jnp.zeros((left_rows.shape[0], F), jnp.float32)
    cross_imag = jnp.zeros((left_rows.shape[0], F), jnp.float32)
    for segment in range(segments):
        left_real = left_float[:, segment, 0]
        left_imag = left_float[:, segment, 1]
        right_real = right_float[:, segment, 0]
        right_imag = right_float[:, segment, 1]
        cross_real = cross_real + (left_real * right_real + left_imag * right_imag)
        cross_imag = cross_imag + (left_imag * right_real - left_real * right_imag)
    inverse = 1.0 / segments
    return (cross_real * inverse, cross_imag * inverse)


def outer_lags(left_rows, right_rows, tables):
    cross_real, cross_imag = outer_cross(left_rows, right_rows)
    return cross_to_lags(cross_real, cross_imag, tables).reshape(
        left_rows.shape[0], right_rows.shape[0], LAGS
    )


def on_device(spectra, source_pick, pair_remote, pair_local, pair_count):
    white = whiten(spectra)
    channels_here = white.shape[0]
    flattened = white.reshape(channels_here, -1)
    tables = lag_tables()
    channel_ids = jnp.arange(channels_here, dtype=jnp.int32)
    picker = (channel_ids[None, :] == source_pick[:, None]).astype(jnp.bfloat16)
    source = jnp.dot(picker, flattened, preferred_element_type=jnp.float32).astype(jnp.bfloat16)
    source = source.reshape((1,) + white.shape[1:])

    def correlate(shard_rows):
        rows_here = shard_rows.shape[0]
        if rows_here > source_block and rows_here % source_block == 0:
            portions = shard_rows.reshape(
                (rows_here // source_block, source_block) + shard_rows.shape[1:]
            )
            result = lax.map(lambda portion: outer_lags(white, portion, tables), portions)
            return jnp.transpose(result, (1, 0, 2, 3)).reshape(channels_here, rows_here, LAGS)
        return outer_lags(white, shard_rows, tables)

    group_corr = correlate(lax.all_gather(source, "dev", axis=0, tiled=True))
    groups = lax.axis_size("grp")
    remote_ids = pair_remote.reshape(groups, -1)
    local_ids = pair_local.reshape(groups, -1)
    slot_count = remote_ids.shape[1]
    gathered = lax.all_gather(white[None], "grp", axis=0, tiled=True)
    remote_picker = (remote_ids[:, :, None] == channel_ids[None, None, :]).astype(jnp.bfloat16)
    remote_rows = jnp.einsum(
        "hkc,hcx->hkx",
        remote_picker,
        gathered.reshape(groups, channels_here, -1),
        preferred_element_type=jnp.float32,
    ).astype(jnp.bfloat16)
    local_picker = (local_ids.reshape(-1)[:, None] == channel_ids[None, :]).astype(jnp.bfloat16)
    local_rows = jnp.dot(local_picker, flattened, preferred_element_type=jnp.float32).astype(
        jnp.bfloat16
    )
    cross_real, cross_imag = pair_cross(
        local_rows.reshape((-1,) + white.shape[1:]), remote_rows.reshape((-1,) + white.shape[1:])
    )
    lags_out = cross_to_lags(cross_real, cross_imag, tables).reshape(groups, slot_count, LAGS)
    valid_mask = (jnp.arange(slot_count)[None, :] < pair_count.reshape(groups, 1)).astype(
        jnp.float32
    )
    cross_corr = (lags_out * valid_mask[:, :, None]).reshape(1, 1, groups, slot_count, LAGS)
    return (group_corr, cross_corr)


def solution(mesh):
    return jax.shard_map(
        on_device,
        mesh=mesh,
        in_specs=(
            P(("grp", "dev"), None, None, None),
            P(("grp", "dev")),
            P("grp", "dev", None, None),
            P("grp", "dev", None, None),
            P("grp", "dev", None),
        ),
        out_specs=(P(("grp", "dev"), None, None), P("grp", "dev", None, None, None)),
        check_vma=False,
    )
```

profile of v0, /device:TPU:0, one launch (start us, length us, event | category | flops | bytes accessed | tf_op | source)
XLA Modules:
  0.0 193.5 jit_solution(853574657091264866)
XLA Ops:
  1.3 0.8 eq.73
  2.0 0.7 compare_select_fusion
  3.0 1.4 copy.52
  6.3 24.6 %all_gather.6 = bf16[16,2,2,4096]{3,2,1,0:T(2,128)(2,1)S(1)} all-gather(bf16[1,2,2,4096]{3,2,1,0:T(2,128)(2,1)S(1)} %reshape.266), channel_id=1, replica_groups=mesh['grp'=2,'dev'=16] {'dev'}, dimensions={0}, use_global_device_ids=true | all-gather | bytes 557056 | tf_op jit(solution)/shard_map/all_gather | solution.py:115
  30.9 9.4 %all-gather = bf16[16,2,2,4096]{3,0,2,1:T(8,128)(2,1)S(1)} all-gather(bf16[8,2,2,4096]{3,0,2,1:T(8,128)(2,1)S(1)} %get-tuple-element.3), channel_id=2, replica_groups=mesh['grp'=2,'dev'=16] {'grp'}, dimensions={0}, use_global_device_ids=true | all-gather | bytes 786432 | tf_op jit(solution)/shard_map/all_gather | solution.py:120
  42.4 9.9 %fusion.25 = f32[4,128]{1,0:T(4,128)S(1)} fusion(f32[4,1,1,4096]{3,0,2,1:T(4,128)S(1)} %get-tuple-element.19, f32[4,1,1,4096]{3,0,2,1:T(4,128)S(1)} %get-tuple-element.18, f32[4096]{0:T(1024)S(1)} %get-tuple-element.38, f32[4096]{0:T(1024)S(1)} %get-tuple-element.39), kind=kOutput, calls=%fused_computation.58 | convolution fusion | flops 12124160 | bytes 165888 | tf_op jit(solution)/shard_map/dot_general | solution.py:48
  52.3 10.0 %convolution_add_fusion.6 = f32[4,128]{1,0:T(4,128)S(1)} fusion(f32[4,128]{1,0:T(4,128)S(1)} %fusion.25, f32[4,1,1,4096]{3,0,2,1:T(4,128)S(1)} %get-tuple-element.19, f32[4,1,1,4096]{3,0,2,1:T(4,128)S(1)} %get-tuple-element.18, f32[4096]{0:T(1024)S(1)} %get-tuple-element.38, f32[4096]{0:T(1024)S(1)} %get-tuple-element.39), kind=kOutput, calls=%fused_computation.54 | convolution fusion | flops 12648960 | bytes 167936 | tf_op jit(solution)/shard_map/dot_general | solution.py:49
  62.3 9.9 %fusion.24 = f32[4,128]{1,0:T(4,128)S(1)} fusion(f32[4,1,1,4096]{3,0,2,1:T(4,128)S(1)} %get-tuple-element.19, f32[4,1,1,4096]{3,0,2,1:T(4,128)S(1)} %get-tuple-element.18), kind=kOutput, calls=%fused_computation.57 | convolution fusion | flops 12124160 | bytes 133120 | tf_op jit(solution)/shard_map/dot_general | solution.py:48
  72.2 10.0 %convolution_add_fusion.5 = f32[4,128]{1,0:T(4,128)S(1)} fusion(f32[4,128]{1,0:T(4,128)S(1)} %fusion.24, f32[4,1,1,4096]{3,0,2,1:T(4,128)S(1)} %get-tuple-element.19, f32[4,1,1,4096]{3,0,2,1:T(4,128)S(1)} %get-tuple-element.18), kind=kOutput, calls=%fused_computation.53 | convolution fusion | flops 12648960 | bytes 135168 | tf_op jit(solution)/shard_map/dot_general | solution.py:49
  82.2 9.9 %fusion.23 = f32[4,128]{1,0:T(4,128)S(1)} fusion(f32[4,1,1,4096]{3,0,2,1:T(4,128)S(1)} %get-tuple-element.19, f32[4,1,1,4096]{3,0,2,1:T(4,128)S(1)} %get-tuple-element.18, f32[4096]{0:T(1024)S(1)} %get-tuple-element.36, f32[4096]{0:T(1024)S(1)} %get-tuple-element.37), kind=kOutput, calls=%fused_computation.56 | convolution fusion | flops 12124160 | bytes 165888 | tf_op jit(solution)/shard_map/dot_general | solution.py:48
  92.1 10.0 %convolution_add_fusion.4 = f32[4,128]{1,0:T(4,128)S(1)} fusion(f32[4,128]{1,0:T(4,128)S(1)} %fusion.23, f32[4,1,1,4096]{3,0,2,1:T(4,128)S(1)} %get-tuple-element.19, f32[4,1,1,4096]{3,0,2,1:T(4,128)S(1)} %get-tuple-element.18, f32[4096]{0:T(1024)S(1)} %get-tuple-element.36, f32[4096]{0:T(1024)S(1)} %get-tuple-element.37), kind=kOutput, calls=%fused_computation.52 | convolution fusion | flops 12648960 | bytes 167936 | tf_op jit(solution)/shard_map/dot_general | solution.py:49
  102.1 9.9 %fusion.26 = f32[4,128]{1,0:T(4,128)S(1)} fusion(f32[4,1,1,4096]{3,0,2,1:T(4,128)S(1)} %get-tuple-element.19, f32[4,1,1,4096]{3,0,2,1:T(4,128)S(1)} %get-tuple-element.18, f32[4096]{0:T(1024)S(1)} %get-tuple-element.40, f32[4096]{0:T(1024)S(1)} %get-tuple-element.41), kind=kOutput, calls=%fused_computation.59 | convolution fusion | flops 12124160 | bytes 165888 | tf_op jit(solution)/shard_map/dot_general | solution.py:48
  111.9 10.0 %convolution_add_fusion.7 = f32[4,128]{1,0:T(4,128)S(1)} fusion(f32[4,128]{1,0:T(4,128)S(1)} %fusion.26, f32[4,1,1,4096]{3,0,2,1:T(4,128)S(1)} %get-tuple-element.19, f32[4,1,1,4096]{3,0,2,1:T(4,128)S(1)} %get-tuple-element.18, f32[4096]{0:T(1024)S(1)} %get-tuple-element.40, f32[4096]{0:T(1024)S(1)} %get-tuple-element.41), kind=kOutput, calls=%fused_computation.55 | convolution fusion | flops 12648960 | bytes 167936 | tf_op jit(solution)/shard_map/dot_general | solution.py:49
  122.6 1.2 fusion.153
  124.4 1.0 add_add_fusion
  125.4 2.6 %fusion.7 = (bf16[128,4096]{1,0:T(8,128)(2,1)S(1)}, bf16[128,4096]{1,0:T(8,128)(2,1)S(1)}, bf16[128,4096]{1,0:T(8,128)(2,1)S(1)}, bf16[128,4096]{1,0:T(8,128)(2,...) fusion(f32[8,16,4096]{2,1,0:T(8,128)S(1)} %get-tuple-element.17, ...), kind=kLoop, calls=%fused_computation.20 | loop fusion | flops 16777216 | bytes 12681216 | tf_op jit(solution)/shard_map/convert_element_type | solution.py:46
  128.0 7.8 %fusion.30 = f32[128,128]{1,0:T(8,128)S(1)} fusion(bf16[128,4096]{1,0:T(8,128)(2,1)S(1)} %get-tuple-element.5), kind=kOutput, calls=%fused_computation.63 | convolution fusion | flops 142082048 | bytes 1114112 | tf_op jit(solution)/shard_map/dot_general | solution.py:48
  135.8 8.4 %convolution_add_fusion.3 = f32[128,128]{1,0:T(8,128)S(1)} fusion(f32[128,128]{1,0:T(8,128)S(1)} %fusion.30, bf16[128,4096]{1,0:T(8,128)(2,1)S(1)} %get-tuple-element.4), kind=kOutput, calls=%fused_computation.51 | convolution fusion | flops 142622720 | bytes 1179648 | tf_op jit(solution)/shard_map/dot_general | solution.py:49
  144.2 8.0 %fusion.29 = f32[128,128]{1,0:T(8,128)S(1)} fusion(bf16[128,4096]{1,0:T(8,128)(2,1)S(1)} %get-tuple-element.10), kind=kOutput, calls=%fused_computation.62 | convolution fusion | flops 142082048 | bytes 1114112 | tf_op jit(solution)/shard_map/dot_general | solution.py:48
  152.2 8.0 %convolution_add_fusion.2 = f32[128,128]{1,0:T(8,128)S(1)} fusion(f32[128,128]{1,0:T(8,128)S(1)} %fusion.29, bf16[128,4096]{1,0:T(8,128)(2,1)S(1)} %get-tuple-element.11), kind=kOutput, calls=%fused_computation.50 | convolution fusion | flops 142622720 | bytes 1179648 | tf_op jit(solution)/shard_map/dot_general | solution.py:49
  160.2 8.0 %fusion.28 = f32[128,128]{1,0:T(8,128)S(1)} fusion(bf16[128,4096]{1,0:T(8,128)(2,1)S(1)} %get-tuple-element.12), kind=kOutput, calls=%fused_computation.61 | convolution fusion | flops 142082048 | bytes 1114112 | tf_op jit(solution)/shard_map/dot_general | solution.py:48
  168.2 8.4 %convolution_add_fusion.1 = f32[128,128]{1,0:T(8,128)S(1)} fusion(f32[128,128]{1,0:T(8,128)S(1)} %fusion.28, bf16[128,4096]{1,0:T(8,128)(2,1)S(1)} %get-tuple-element.13), kind=kOutput, calls=%fused_computation.49 | convolution fusion | flops 142622720 | bytes 1179648 | tf_op jit(solution)/shard_map/dot_general | solution.py:49
  176.6 7.8 %fusion.27 = f32[128,128]{1,0:T(8,128)S(1)} fusion(bf16[128,4096]{1,0:T(8,128)(2,1)S(1)} %get-tuple-element.14), kind=kOutput, calls=%fused_computation.60 | convolution fusion | flops 142082048 | bytes 1114112 | tf_op jit(solution)/shard_map/dot_general | solution.py:48
  184.4 8.1 %convolution_add_fusion = f32[128,128]{1,0:T(8,128)S(1)} fusion(f32[128,128]{1,0:T(8,128)S(1)} %fusion.27, bf16[128,4096]{1,0:T(8,128)(2,1)S(1)} %get-tuple-element.15), kind=kOutput, calls=%fused_computation.48 | convolution fusion | flops 142622720 | bytes 1179648 | tf_op jit(solution)/shard_map/dot_general | solution.py:49
  (30 shorter events, 6.1 us)
Async XLA Ops:
  3.0 2.4 %copy-start = (f32[8,2,2,4096]{3,2,1,0:T(2,128)S(1)}, f32[8,2,2,4096]{3,2,1,0:T(2,128)}, u32[]{:S(2)}) copy-start(f32[8,2,2,4096]{3,2,1,0:T(2,128)} %param.5) | copy-start | bytes 1572868
  6.0 35.3 %copy-start.1 = (s32[1,1,2,2]{3,2,1,0:T(2,128)S(1)}, s32[1,1,2,2]{3,2,1,0:T(2,128)}, u32[]{:S(2)}) copy-start(s32[1,1,2,2]{3,2,1,0:T(2,128)} %param.7) | copy-start | bytes 52
where the time goes:
time: 196 us; the launch traced here: 193 us
  matrix products  145 us (74%)
  blocking collectives  34 us (17%)
  other arithmetic  6.8 us (3%)
  local copies, waits for them, and re-layouts  6.14 us (3%)
    dot_general x8, matrix products, cross_to_lags(): jnp.dot(rot_imag, sin_table, preferred_element_type=jnp.float32)  72.8 us
    dot_general x8, matrix products, cross_to_lags(): jnp.dot(rot_real, cos_table, preferred_element_type=jnp.float32)  71.2 us
    all_gather x1, blocking collectives, on_device(): group_corr = correlate(lax.all_gather(source, 'dev', axis=0, tiled=True))  24.6 us
    all_gather x1, blocking collectives, on_device(): gathered = lax.all_gather(white[None], 'grp', axis=0, tiled=True)  9.39 us

commit v1 on v0

v1 whole, which is shorter than its diff:
```python
import functools

import jax
import jax.numpy as jnp
import numpy as np
from jax import lax
from jax.experimental import pallas as pl
from jax.experimental.pallas import tpu as pltpu
from jax.sharding import PartitionSpec as P

MESH = pl.DeviceIdType.MESH
F = 4096
LAGS = 512
LAG_BLK = 128
BAND = 64
FINE = 64
CHUNKS = 4
WIDE = F // CHUNKS
LANES = 128


def phase_tables():
    a = np.arange(F // FINE)[:, None] * np.arange(LAG_BLK)[None, :]
    coarse = np.pi * (a * FINE % (2 * F)) / F
    b = np.arange(FINE)[:, None] * (np.arange(LAGS) - LAGS // 2)[None, :]
    fine = np.pi * (b % (2 * F)) / F
    return (
        np.stack([np.cos(coarse), np.sin(coarse)]).astype(np.float32),
        np.stack([np.cos(fine), np.sin(fine)]).astype(np.float32),
    )


def kernel(
    groups, n_dev, slots, channels, pair_rows,
    pick_ref, remote_ref, local_ref, count_ref, x_hbm, coarse_ref, fine_ref,
    group_out, cross_out,
    white, mag, gathered, row_scratch, src_f32, cos_t, sin_t, xr, xi, pr, pi, acc,
    req_out, req_in, rows_out, rows_in,
    load_sem, send_sem, recv_sem, req_send, req_recv, row_send, row_recv,
):
    g = lax.axis_index("grp")
    d = lax.axis_index("dev")
    rows = n_dev // 4
    r, c, k = d // 4, (d // 2) % 2, d % 2
    flip_c = r * 4 + (1 - c) * 2 + k
    flip_k = r * 4 + c * 2 + (1 - k)

    def row_of(t):
        return lax.rem(r + t, rows)

    def group_of(t):
        return lax.rem(g + t, groups)

    loads = []
    for s in range(2):
        for p in range(2):
            copy = pltpu.make_async_copy(x_hbm.at[:, s, p, :], white.at[s * 2 + p], load_sem.at[s * 2 + p])
            copy.start()
            loads.append(copy)

    barrier = pltpu.get_barrier_semaphore()
    for t in range(1, rows):
        pl.semaphore_signal(barrier, inc=1, device_id=(g, row_of(t) * 4 + c * 2 + k), device_id_type=MESH)
    pl.semaphore_signal(barrier, inc=1, device_id=(g, flip_c), device_id_type=MESH)
    pl.semaphore_signal(barrier, inc=1, device_id=(g, flip_k), device_id_type=MESH)
    for t in range(1, groups):
        pl.semaphore_signal(barrier, inc=1, device_id=(group_of(t), d), device_id_type=MESH)

    for t in range(1, groups):
        h = group_of(t)
        for slot in range(slots):
            req_out[t, slot:slot + 1, :] = jnp.full((1, LANES), remote_ref[0, 0, h, slot], jnp.int32)

    pl.semaphore_wait(barrier, rows + 1 + groups - 1)

    started = []

    def remote(src, dst, send, recv, target):
        return pltpu.make_async_remote_copy(
            src_ref=src, dst_ref=dst, send_sem=send, recv_sem=recv, device_id=target, device_id_type=MESH
        )

    for t in range(1, groups):
        copy = remote(req_out.at[t], req_in.at[g], req_send.at[t], req_recv.at[g], (group_of(t), d))
        copy.start()
        started.append(copy)

    for copy in loads:
        copy.wait()

    lane_i = lax.broadcasted_iota(jnp.int32, (LANES, LANES), 0)
    lane_j = lax.broadcasted_iota(jnp.int32, (LANES, LANES), 1)
    averaging = jnp.where(lane_i // BAND == lane_j // BAND, 1.0 / BAND, 0.0).astype(jnp.bfloat16)
    for s in range(2):
        for l in range(F // LANES):
            cols = slice(l * LANES, (l + 1) * LANES)
            re, im = white[2 * s, :, cols], white[2 * s + 1, :, cols]
            mag[l * channels:(l + 1) * channels, :] = jnp.sqrt(re * re + im * im)
        value = mag[...]
        high = value.astype(jnp.bfloat16)
        rest = value - high.astype(jnp.float32)
        mid = rest.astype(jnp.bfloat16)
        low = (rest - mid.astype(jnp.float32)).astype(jnp.bfloat16)
        mean = (
            jnp.dot(high, averaging, preferred_element_type=jnp.float32)
            + jnp.dot(mid, averaging, preferred_element_type=jnp.float32)
            + jnp.dot(low, averaging, preferred_element_type=jnp.float32)
        )
        mag[...] = 1.0 / (mean + 1e-05)
        for l in range(F // LANES):
            cols = slice(l * LANES, (l + 1) * LANES)
            inverse = mag[l * channels:(l + 1) * channels, :]
            for p in range(2):
                scaled = white[2 * s + p, :, cols] * inverse
                white[2 * s + p, :, cols] = scaled.astype(jnp.bfloat16).astype(jnp.float32)

    def pick_row(channel):
        for sp in range(4):
            for q in range(CHUNKS):
                row_scratch[sp * CHUNKS + q:sp * CHUNKS + q + 1, :] = white[
                    sp, pl.ds(channel, 1), q * WIDE:(q + 1) * WIDE
                ]

    pick_row(pick_ref[0])
    gathered[d] = row_scratch[...].astype(jnp.bfloat16)

    n_sent = [0]

    def forward(j, target):
        copy = remote(gathered.at[j], gathered.at[j], send_sem.at[n_sent[0]], recv_sem.at[j], (g, target))
        n_sent[0] += 1
        copy.start()
        started.append(copy)

    def arrived(j):
        remote(gathered.at[j], gathered.at[j], send_sem.at[0], recv_sem.at[j], (g, flip_k)).wait_recv()

    for t in range(1, rows):
        forward(d, row_of(t) * 4 + c * 2 + k)
    forward(d, flip_c)
    forward(d, flip_k)

    channel_id = lax.broadcasted_iota(jnp.int32, (channels, LANES), 0)
    for t in range(1, groups):
        h = group_of(t)
        remote(req_out.at[t], req_in.at[h], req_send.at[t], req_recv.at[h], (h, d)).wait_recv()
        asked = req_in[h]
        for slot in range(slots):
            chosen = channel_id == jnp.broadcast_to(asked[slot:slot + 1, :], (channels, LANES))
            chosen = jnp.concatenate([chosen] * (WIDE // LANES), axis=1)
            for sp in range(4):
                for q in range(CHUNKS):
                    part = jnp.where(chosen, white[sp, :, q * WIDE:(q + 1) * WIDE], 0.0)
                    row_scratch[sp * CHUNKS + q:sp * CHUNKS + q + 1, :] = jnp.sum(part, axis=0, keepdims=True)
            rows_out[t, slot * 16:(slot + 1) * 16, :] = row_scratch[...].astype(jnp.bfloat16)
        copy = remote(rows_out.at[t], rows_in.at[g], row_send.at[t], row_recv.at[g], (h, d))
        copy.start()
        started.append(copy)

    coarse_rows = F // FINE

    def table_part(first, last):
        @pl.loop(first, last)
        def _(a):
            ac, asin = coarse_ref[0, pl.ds(a, 1), :], coarse_ref[1, pl.ds(a, 1), :]
            here = pl.ds(pl.multiple_of(a * FINE, FINE), FINE)
            for l in range(LAGS // LANES):
                cols = slice(l * LANES, (l + 1) * LANES)
                bc, bs = fine_ref[0, :, cols], fine_ref[1, :, cols]
                cos_t[here, cols] = (ac * bc - asin * bs).astype(jnp.bfloat16)
                sin_t[here, cols] = (-(asin * bc + ac * bs)).astype(jnp.bfloat16)

    for t in range(rows):
        table_part(coarse_rows * t // rows, coarse_rows * (t + 1) // rows)
        if t > 0:
            j = row_of(t) * 4 + c * 2 + k
            arrived(j)
            forward(j, flip_c)
            forward(j, flip_k)
            j = row_of(t - 1) * 4 + (1 - c) * 2 + k
            arrived(j)
            forward(j, flip_k)
    j = row_of(rows - 1) * 4 + (1 - c) * 2 + k
    arrived(j)
    forward(j, flip_k)

    def cross_chip(first):
        for half in range(2):
            src_f32[half] = gathered[first + half].astype(jnp.float32)
        base = pl.multiple_of(first * channels, 2 * channels)

        for q in range(CHUNKS):
            for l in range(WIDE // LANES):
                cols = slice(q * WIDE + l * LANES, q * WIDE + (l + 1) * LANES)
                lanes = slice(l * LANES, (l + 1) * LANES)
                w = [white[sp, :, cols] for sp in range(4)]
                real, imag = [], []
                for half in range(2):
                    v = [
                        jnp.broadcast_to(
                            src_f32[half, sp * CHUNKS + q:sp * CHUNKS + q + 1, lanes], (channels, LANES)
                        )
                        for sp in range(4)
                    ]
                    real.append(w[0] * v[0] + w[1] * v[1] + w[2] * v[2] + w[3] * v[3])
                    imag.append(w[1] * v[0] - w[0] * v[1] + w[3] * v[2] - w[2] * v[3])
                xr[pl.ds(base, 2 * channels), cols] = jnp.concatenate(real, axis=0).astype(jnp.bfloat16)
                xi[pl.ds(base, 2 * channels), cols] = jnp.concatenate(imag, axis=0).astype(jnp.bfloat16)

    @pl.loop(0, rows)
    def _(t):
        arrived(row_of(t) * 4 + c * 2 + (1 - k))
        cross_chip(row_of(t) * 4 + c * 2)
        arrived(row_of(t) * 4 + (1 - c) * 2 + (1 - k))
        cross_chip(row_of(t) * 4 + (1 - c) * 2)

    if pair_rows:
        pr[...] = jnp.zeros_like(pr)
        pi[...] = jnp.zeros_like(pi)
    for t in range(1, groups):
        h = group_of(t)
        remote(rows_out.at[t], rows_in.at[h], row_send.at[t], row_recv.at[h], (h, d)).wait_recv()
        for slot in range(slots):
            pick_row(local_ref[0, 0, h, slot])
            there = rows_in[h, slot * 16:(slot + 1) * 16, :].astype(jnp.float32)
            here = row_scratch[...]
            w = [here[sp * CHUNKS:(sp + 1) * CHUNKS] for sp in range(4)]
            v = [there[sp * CHUNKS:(sp + 1) * CHUNKS] for sp in range(4)]
            real = w[0] * v[0] + w[1] * v[1] + w[2] * v[2] + w[3] * v[3]
            imag = w[1] * v[0] - w[0] * v[1] + w[3] * v[2] - w[2] * v[3]
            row = (t - 1) * slots + slot
            for q in range(CHUNKS):
                pr[row:row + 1, q * WIDE:(q + 1) * WIDE] = real[q:q + 1]
                pi[row:row + 1, q * WIDE:(q + 1) * WIDE] = imag[q:q + 1]
    if pair_rows:
        xr[n_dev * channels:, :] = pr[...].astype(jnp.bfloat16)
        xi[n_dev * channels:, :] = pi[...].astype(jnp.bfloat16)

    acc[...] = jnp.zeros_like(acc)
    depth = 1024

    @pl.loop(0, F // depth)
    def _(step):
        here = pl.ds(pl.multiple_of(step * depth, depth), depth)
        acc[...] += jnp.dot(xr[:, here], cos_t[here, :], preferred_element_type=jnp.float32) + jnp.dot(
            xi[:, here], sin_t[here, :], preferred_element_type=jnp.float32
        )

    scale = 0.5 * F ** (-0.5)
    group_out[...] = acc[:n_dev * channels, :].reshape(n_dev, channels, LAGS) * scale
    cross_out[g] = jnp.zeros((slots, LAGS), jnp.float32)
    for t in range(1, groups):
        h = group_of(t)
        for slot in range(slots):
            row = n_dev * channels + (t - 1) * slots + slot
            valid = jnp.where(slot < count_ref[0, 0, h], scale, 0.0)
            cross_out[h, slot:slot + 1, :] = acc[row:row + 1, :] * valid

    for copy in started:
        copy.wait_send()


def solution(mesh):
    groups, n_dev = mesh.shape["grp"], mesh.shape["dev"]
    coarse, fine = phase_tables()

    def on_device(spectra, source_pick, pair_remote, pair_local, pair_count):
        channels = spectra.shape[0]
        slots = pair_remote.shape[3]
        pair_rows = -(-((groups - 1) * slots) // 16) * 16
        total = n_dev * channels + pair_rows
        smem = pl.BlockSpec(memory_space=pltpu.SMEM)
        vmem = pl.BlockSpec(memory_space=pltpu.VMEM)
        f32, bf16 = jnp.float32, jnp.bfloat16
        group_corr, cross_corr = pl.pallas_call(
            functools.partial(kernel, groups, n_dev, slots, channels, pair_rows),
            out_shape=(
                jax.ShapeDtypeStruct((n_dev, channels, LAGS), f32),
                jax.ShapeDtypeStruct((groups, slots, LAGS), f32),
            ),
            in_specs=[smem, smem, smem, smem, pl.BlockSpec(memory_space=pl.ANY), vmem, vmem],
            out_specs=(vmem, vmem),
            scratch_shapes=[
                pltpu.VMEM((4, channels, F), f32),
                pltpu.VMEM((F // LANES * channels, LANES), f32),
                pltpu.VMEM((n_dev, 16, WIDE), bf16),
                pltpu.VMEM((16, WIDE), f32),
                pltpu.VMEM((2, 16, WIDE), f32),
                pltpu.VMEM((F, LAGS), bf16),
                pltpu.VMEM((F, LAGS), bf16),
                pltpu.VMEM((total, F), bf16),
                pltpu.VMEM((total, F), bf16),
                pltpu.VMEM((16, F), f32),
                pltpu.VMEM((16, F), f32),
                pltpu.VMEM((total, LAGS), f32),
                pltpu.VMEM((groups, 8, LANES), jnp.int32),
                pltpu.VMEM((groups, 8, LANES), jnp.int32),
                pltpu.VMEM((groups, slots * 16, WIDE), bf16),
                pltpu.VMEM((groups, slots * 16, WIDE), bf16),
                pltpu.SemaphoreType.DMA((4,)),
                pltpu.SemaphoreType.DMA((n_dev,)),
                pltpu.SemaphoreType.DMA((n_dev,)),
                pltpu.SemaphoreType.DMA((groups,)),
                pltpu.SemaphoreType.DMA((groups,)),
                pltpu.SemaphoreType.DMA((groups,)),
                pltpu.SemaphoreType.DMA((groups,)),
            ],
            compiler_params=pltpu.CompilerParams(
                collective_id=0, has_side_effects=True, vmem_limit_bytes=56 << 20
            ),
        )(source_pick, pair_remote, pair_local, pair_count, spectra, jnp.asarray(coarse), jnp.asarray(fine))
        return (
            jnp.transpose(group_corr, (1, 0, 2)),
            cross_corr.reshape(1, 1, groups, slots, LAGS),
        )

    return jax.shard_map(
        on_device,
        mesh=mesh,
        in_specs=(
            P(("grp", "dev"), None, None, None),
            P(("grp", "dev")),
            P("grp", "dev", None, None),
            P("grp", "dev", None, None),
            P("grp", "dev", None),
        ),
        out_specs=(P(("grp", "dev"), None, None), P("grp", "dev", None, None, None)),
        check_vma=False,
    )
```

time: 196 us -> 25.7 us (0.13); the launches traced: 193 us -> 25.6 us
  matrix products: 145 us -> 0 us
  blocking collectives: 34 us -> 0 us
  Pallas kernels: 0 us -> 21.9 us
  other arithmetic: 6.8 us -> 0 us
  local copies, waits for them, and re-layouts: 6.14 us -> 2.42 us
    dot_general x19 -> x0, matrix products: 145 us -> none  [the longest x8 72.8 us: cross_to_lags(): jnp.dot(rot_imag, sin_table, preferred_element_type=jnp.float32)]
    all_gather x2 -> x0, blocking collectives: 34 us -> none  [the longest x1 24.6 us: on_device(): group_corr = correlate(lax.all_gather(source, 'dev', axis=0, tiled=True))]
    pallas_call x0 -> x1, Pallas kernels: none -> 21.9 us  [on_device(): pl.pallas_call(functools.partial(kernel, groups, n_dev, slots, channels,...]
    convert_element_type x4 -> x0, other arithmetic: 2.96 us -> none  [the longest x1 2.6 us: cross_to_lags(): (cross_real * turn_sin + cross_imag * turn_cos).astype(jnp.bfloat16)]
    mul x6 -> x0, other arithmetic: 2.39 us -> none  [the longest x2 1.41 us: on_device(): lags_out * valid_mask[:, :, None]]
where the time goes in v1:
time: 25.7 us; the launch traced here: 25.6 us
  Pallas kernels  21.9 us (85%)
  local copies, waits for them, and re-layouts  2.42 us (9%)
  between operations  1.29 us (5%)
    pallas_call x1, Pallas kernels, on_device(): pl.pallas_call(functools.partial(kernel, groups, n_dev, slots, channels,...  21.9 us
    unnamed x4, local copies, waits for them, and re-layouts  2.42 us

profile of v1, /device:TPU:0, one launch (start us, length us, event | category | flops | bytes accessed | tf_op | source)
XLA Modules:
  0.0 25.6 jit_solution(16786454878395472870)
XLA Ops:
  1.3 21.9 %shard_map.86 = (f32[16,8,512]{2,1,0:T(8,128)}, f32[2,2,512]{2,1,0:T(2,128)}) custom-call(s32[1]{0:T(128)S(6)} %copy.11.pick_ref, s32[1,1,2,2]{3,2,1,0:T(2,128)} %remote_ref.1, s32[1,1,2,2]{3,2,1,0:T(2,128)} %local_ref.1, s32[1,1,2]{2,1,0:T(1,128)} %count_ref.1, f32[8,2,2,4096]{3,2,1,0:T(2,128)} %x_hbm.1, f32[2,64,128]{2,1,0:T(8,128)} %constant.4.clone.coarse_ref, ...), custom_call_target="tpu_custom_call" | custom-call | tf_op jit(solution)/shard_map/pallas_call | solution.py:275
  23.2 0.0 copy-start
  23.2 1.8 %copy.9 = f32[8,16,512]{2,1,0:T(8,128)} copy(f32[8,16,512]{2,0,1:T(8,128)} %bitcast.2) | data formatting | bytes 524288
  25.0 0.0 copy-done
  25.0 0.6 %copy.12 = f32[1,1,2,2,512]{4,3,2,1,0:T(2,128)} copy(f32[1,1,2,2,512]{4,3,2,1,0:T(2,128)S(1)} %bitcast.3) | data formatting | bytes 16384
Async XLA Ops:
  23.2 1.8 %copy-start = (f32[2,2,512]{2,1,0:T(2,128)S(1)}, f32[2,2,512]{2,1,0:T(2,128)}, u32[]{:S(2)}) copy-start(f32[2,2,512]{2,1,0:T(2,128)} %get-tuple-element.5) | copy-start | bytes 24580

commit v2 on v1

--- a/solution.py
+++ b/solution.py
@@ -17,6 +17,8 @@
 CHUNKS = 4
 WIDE = F // CHUNKS
 LANES = 128
+PARTS = 2
+PART = F // PARTS
 
 
 def phase_tables():
@@ -32,11 +34,11 @@
 
 def kernel(
     groups, n_dev, slots, channels, pair_rows,
-    pick_ref, remote_ref, local_ref, count_ref, x_hbm, coarse_ref, fine_ref,
+    pick_ref, remote_ref, local_ref, count_ref, x_hbm, coarse_hbm, fine_hbm,
     group_out, cross_out,
-    white, mag, gathered, row_scratch, src_f32, cos_t, sin_t, xr, xi, pr, pi, acc,
+    raw, white, mag, gathered, row_scratch, src_f32, cos_t, sin_t, xr, xi, pr, pi, acc,
     req_out, req_in, rows_out, rows_in,
-    load_sem, send_sem, recv_sem, req_send, req_recv, row_send, row_recv,
+    coarse_ref, fine_ref, load_sem, table_sem, send_sem, recv_sem, req_send, req_recv, row_send, row_recv,
 ):
     g = lax.axis_index("grp")
     d = lax.axis_index("dev")
@@ -52,11 +54,19 @@
         return lax.rem(g + t, groups)
 
     loads = []
-    for s in range(2):
-        for p in range(2):
-            copy = pltpu.make_async_copy(x_hbm.at[:, s, p, :], white.at[s * 2 + p], load_sem.at[s * 2 + p])
-            copy.start()
-            loads.append(copy)
+    for q in range(PARTS):
+        cols = pl.ds(q * PART, PART)
+        for sp in range(4):
+            loads.append(pltpu.make_async_copy(
+                x_hbm.at[:, sp // 2, sp % 2, cols], raw.at[sp, :, cols], load_sem.at[q * 4 + sp]
+            ))
+            loads[-1].start()
+    table_loads = [
+        pltpu.make_async_copy(coarse_hbm, coarse_ref, table_sem.at[0]),
+        pltpu.make_async_copy(fine_hbm, fine_ref, table_sem.at[1]),
+    ]
+    for copy in table_loads:
+        copy.start()
 
     barrier = pltpu.get_barrier_semaphore()
     for t in range(1, rows):
@@ -71,8 +81,6 @@
         for slot in range(slots):
             req_out[t, slot:slot + 1, :] = jnp.full((1, LANES), remote_ref[0, 0, h, slot], jnp.int32)
 
-    pl.semaphore_wait(barrier, rows + 1 + groups - 1)
-
     started = []
 
     def remote(src, dst, send, recv, target):
@@ -80,22 +88,20 @@
             src_ref=src, dst_ref=dst, send_sem=send, recv_sem=recv, device_id=target, device_id_type=MESH
         )
 
-    for t in range(1, groups):
-        copy = remote(req_out.at[t], req_in.at[g], req_send.at[t], req_recv.at[g], (group_of(t), d))
-        copy.start()
-        started.append(copy)
-
-    for copy in loads:
-        copy.wait()
-
     lane_i = lax.broadcasted_iota(jnp.int32, (LANES, LANES), 0)
     lane_j = lax.broadcasted_iota(jnp.int32, (LANES, LANES), 1)
     averaging = jnp.where(lane_i // BAND == lane_j // BAND, 1.0 / BAND, 0.0).astype(jnp.bfloat16)
-    for s in range(2):
-        for l in range(F // LANES):
-            cols = slice(l * LANES, (l + 1) * LANES)
-            re, im = white[2 * s, :, cols], white[2 * s + 1, :, cols]
-            mag[l * channels:(l + 1) * channels, :] = jnp.sqrt(re * re + im * im)
+    width = PART // CHUNKS
+
+    def whiten(q):
+        for copy in loads[q * 4:(q + 1) * 4]:
+            copy.wait()
+        tiles = PART // LANES
+        for s in range(2):
+            for l in range(tiles):
+                cols = slice(q * PART + l * LANES, q * PART + (l + 1) * LANES)
+                re, im = raw[2 * s, :, cols], raw[2 * s + 1, :, cols]
+                mag[(s * tiles + l) * channels:(s * tiles + l + 1) * channels, :] = jnp.sqrt(re * re + im * im)
         value = mag[...]
         high = value.astype(jnp.bfloat16)
         rest = value - high.astype(jnp.float32)
@@ -107,38 +113,74 @@
             + jnp.dot(low, averaging, preferred_element_type=jnp.float32)
         )
         mag[...] = 1.0 / (mean + 1e-05)
-        for l in range(F // LANES):
-            cols = slice(l * LANES, (l + 1) * LANES)
-            inverse = mag[l * channels:(l + 1) * channels, :]
-            for p in range(2):
-                scaled = white[2 * s + p, :, cols] * inverse
-                white[2 * s + p, :, cols] = scaled.astype(jnp.bfloat16).astype(jnp.float32)
+        for s in range(2):
+            for l in range(tiles):
+                cols = slice(q * PART + l * LANES, q * PART + (l + 1) * LANES)
+                inverse = mag[(s * tiles + l) * channels:(s * tiles + l + 1) * channels, :]
+                for p in range(2):
+                    scaled = raw[2 * s + p, :, cols] * inverse
+                    white[2 * s + p, :, cols] = scaled.astype(jnp.bfloat16).astype(jnp.float32)
 
     def pick_row(channel):
         for sp in range(4):
-            for q in range(CHUNKS):
-                row_scratch[sp * CHUNKS + q:sp * CHUNKS + q + 1, :] = white[
-                    sp, pl.ds(channel, 1), q * WIDE:(q + 1) * WIDE
+            for i in range(CHUNKS):
+                row_scratch[sp * CHUNKS + i:sp * CHUNKS + i + 1, :] = white[
+                    sp, pl.ds(channel, 1), i * WIDE:(i + 1) * WIDE
                 ]
 
-    pick_row(pick_ref[0])
-    gathered[d] = row_scratch[...].astype(jnp.bfloat16)
+    def pick_source(q):
+        for sp in range(4):
+            for i in range(CHUNKS):
+                first = q * PART + i * width
+                row_scratch[sp * CHUNKS + i:sp * CHUNKS + i + 1, :width] = white[
+                    sp, pl.ds(pick_ref[0], 1), first:first + width
+                ]
+        gathered[q, d] = row_scratch[:, :width].astype(jnp.bfloat16)
 
     n_sent = [0]
 
-    def forward(j, target):
-        copy = remote(gathered.at[j], gathered.at[j], send_sem.at[n_sent[0]], recv_sem.at[j], (g, target))
+    def forward(q, j, target):
+        copy = remote(
+            gathered.at[q, j], gathered.at[q, j], send_sem.at[n_sent[0]], recv_sem.at[q, j], (g, target)
+        )
         n_sent[0] += 1
         copy.start()
         started.append(copy)
 
-    def arrived(j):
-        remote(gathered.at[j], gathered.at[j], send_sem.at[0], recv_sem.at[j], (g, flip_k)).wait_recv()
-
-    for t in range(1, rows):
-        forward(d, row_of(t) * 4 + c * 2 + k)
-    forward(d, flip_c)
-    forward(d, flip_k)
+    def arrived(q, j):
+        remote(gathered.at[q, j], gathered.at[q, j], send_sem.at[0], recv_sem.at[q, j], (g, flip_k)).wait_recv()
+
+    def send_own(q):
+        for t in range(1, rows):
+            forward(q, d, row_of(t) * 4 + c * 2 + k)
+        forward(q, d, flip_c)
+        forward(q, d, flip_k)
+
+    def pass_column(q):
+        for t in range(1, rows):
+            j = row_of(t) * 4 + c * 2 + k
+            arrived(q, j)
+            forward(q, j, flip_c)
+            forward(q, j, flip_k)
+
+    def pass_other(q):
+        for t in range(rows):
+            j = row_of(t) * 4 + (1 - c) * 2 + k
+            arrived(q, j)
+            forward(q, j, flip_k)
+
+    whiten(0)
+    pick_source(0)
+    pl.semaphore_wait(barrier, rows + 1 + groups - 1)
+    send_own(0)
+    for t in range(1, groups):
+        copy = remote(req_out.at[t], req_in.at[g], req_send.at[t], req_recv.at[g], (group_of(t), d))
+        copy.start()
+        started.append(copy)
+    for q in range(1, PARTS):
+        whiten(q)
+        pick_source(q)
+        send_own(q)
 
     channel_id = lax.broadcasted_iota(jnp.int32, (channels, LANES), 0)
     for t in range(1, groups):
@@ -157,6 +199,8 @@
         copy.start()
         started.append(copy)
 
+    for copy in table_loads:
+        copy.wait()
     coarse_rows = F // FINE
 
     def table_part(first, last):
@@ -170,35 +214,21 @@
                 cos_t[here, cols] = (ac * bc - asin * bs).astype(jnp.bfloat16)
                 sin_t[here, cols] = (-(asin * bc + ac * bs)).astype(jnp.bfloat16)
 
-    for t in range(rows):
-        table_part(coarse_rows * t // rows, coarse_rows * (t + 1) // rows)
-        if t > 0:
-            j = row_of(t) * 4 + c * 2 + k
-            arrived(j)
-            forward(j, flip_c)
-            forward(j, flip_k)
-            j = row_of(t - 1) * 4 + (1 - c) * 2 + k
-            arrived(j)
-            forward(j, flip_k)
-    j = row_of(rows - 1) * 4 + (1 - c) * 2 + k
-    arrived(j)
-    forward(j, flip_k)
-
-    def cross_chip(first):
+    def cross_chip(q, first):
         for half in range(2):
-            src_f32[half] = gathered[first + half].astype(jnp.float32)
+            src_f32[half] = gathered[q, first + half].astype(jnp.float32)
         base = pl.multiple_of(first * channels, 2 * channels)
-
-        for q in range(CHUNKS):
-            for l in range(WIDE // LANES):
-                cols = slice(q * WIDE + l * LANES, q * WIDE + (l + 1) * LANES)
+        for i in range(CHUNKS):
+            for l in range(width // LANES):
+                start = q * PART + i * width + l * LANES
+                cols = slice(start, start + LANES)
                 lanes = slice(l * LANES, (l + 1) * LANES)
                 w = [white[sp, :, cols] for sp in range(4)]
                 real, imag = [], []
                 for half in range(2):
                     v = [
                         jnp.broadcast_to(
-                            src_f32[half, sp * CHUNKS + q:sp * CHUNKS + q + 1, lanes], (channels, LANES)
+                            src_f32[half, sp * CHUNKS + i:sp * CHUNKS + i + 1, lanes], (channels, LANES)
                         )
                         for sp in range(4)
                     ]
@@ -207,12 +237,30 @@
                 xr[pl.ds(base, 2 * channels), cols] = jnp.concatenate(real, axis=0).astype(jnp.bfloat16)
                 xi[pl.ds(base, 2 * channels), cols] = jnp.concatenate(imag, axis=0).astype(jnp.bfloat16)
 
-    @pl.loop(0, rows)
-    def _(t):
-        arrived(row_of(t) * 4 + c * 2 + (1 - k))
-        cross_chip(row_of(t) * 4 + c * 2)
-        arrived(row_of(t) * 4 + (1 - c) * 2 + (1 - k))
-        cross_chip(row_of(t) * 4 + (1 - c) * 2)
+    def cross_part(q):
+        @pl.loop(0, rows)
+        def _(t):
+            arrived(q, row_of(t) * 4 + c * 2 + (1 - k))
+            cross_chip(q, row_of(t) * 4 + c * 2)
+
+        @pl.loop(0, rows)
+        def _(t):
+            arrived(q, row_of(t) * 4 + (1 - c) * 2 + (1 - k))
+            cross_chip(q, row_of(t) * 4 + (1 - c) * 2)
+
+    def multiply(q):
+        here = slice(q * PART, (q + 1) * PART)
+        part = jnp.dot(xr[:, here], cos_t[here, :], preferred_element_type=jnp.float32) + jnp.dot(
+            xi[:, here], sin_t[here, :], preferred_element_type=jnp.float32
+        )
+        acc[...] = part if q == 0 else acc[...] + part
+
+    table_part(0, coarse_rows // 2)
+    pass_column(0)
+    table_part(coarse_rows // 2, coarse_rows)
+    for q in range(1, PARTS):
+        pass_column(q)
+        pass_other(q - 1)
 
     if pair_rows:
         pr[...] = jnp.zeros_like(pr)
@@ -236,18 +284,15 @@
         xr[n_dev * channels:, :] = pr[...].astype(jnp.bfloat16)
         xi[n_dev * channels:, :] = pi[...].astype(jnp.bfloat16)
 
-    acc[...] = jnp.zeros_like(acc)
-    depth = 1024
-
-    @pl.loop(0, F // depth)
-    def _(step):
-        here = pl.ds(pl.multiple_of(step * depth, depth), depth)
-        acc[...] += jnp.dot(xr[:, here], cos_t[here, :], preferred_element_type=jnp.float32) + jnp.dot(
-            xi[:, here], sin_t[here, :], preferred_element_type=jnp.float32
-        )
+    for q in range(PARTS):
+        cross_part(q)
+        if q + 1 < PARTS:
+            pass_other(PARTS - 1)
+        multiply(q)
 
     scale = 0.5 * F ** (-0.5)
-    group_out[...] = acc[:n_dev * channels, :].reshape(n_dev, channels, LAGS) * scale
+    for j in range(n_dev):
+        group_out[:, j, :] = acc[j * channels:(j + 1) * channels, :] * scale
     cross_out[g] = jnp.zeros((slots, LAGS), jnp.float32)
     for t in range(1, groups):
         h = group_of(t)
@@ -270,22 +315,24 @@
         pair_rows = -(-((groups - 1) * slots) // 16) * 16
         total = n_dev * channels + pair_rows
         smem = pl.BlockSpec(memory_space=pltpu.SMEM)
+        hbm = pl.BlockSpec(memory_space=pl.ANY)
         vmem = pl.BlockSpec(memory_space=pltpu.VMEM)
         f32, bf16 = jnp.float32, jnp.bfloat16
         group_corr, cross_corr = pl.pallas_call(
             functools.partial(kernel, groups, n_dev, slots, channels, pair_rows),
             out_shape=(
-                jax.ShapeDtypeStruct((n_dev, channels, LAGS), f32),
+                jax.ShapeDtypeStruct((channels, n_dev, LAGS), f32),
                 jax.ShapeDtypeStruct((groups, slots, LAGS), f32),
             ),
-            in_specs=[smem, smem, smem, smem, pl.BlockSpec(memory_space=pl.ANY), vmem, vmem],
+            in_specs=[smem, smem, smem, smem, hbm, hbm, hbm],
             out_specs=(vmem, vmem),
             scratch_shapes=[
                 pltpu.VMEM((4, channels, F), f32),
-                pltpu.VMEM((F // LANES * channels, LANES), f32),
-                pltpu.VMEM((n_dev, 16, WIDE), bf16),
+                pltpu.VMEM((4, channels, F), f32),
+                pltpu.VMEM((2 * PART // LANES * channels, LANES), f32),
+                pltpu.VMEM((PARTS, n_dev, 16, PART // CHUNKS), bf16),
                 pltpu.VMEM((16, WIDE), f32),
-                pltpu.VMEM((2, 16, WIDE), f32),
+                pltpu.VMEM((2, 16, PART // CHUNKS), f32),
                 pltpu.VMEM((F, LAGS), bf16),
                 pltpu.VMEM((F, LAGS), bf16),
                 pltpu.VMEM((total, F), bf16),
@@ -297,9 +344,12 @@
                 pltpu.VMEM((groups, 8, LANES), jnp.int32),
                 pltpu.VMEM((groups, slots * 16, WIDE), bf16),
                 pltpu.VMEM((groups, slots * 16, WIDE), bf16),
-                pltpu.SemaphoreType.DMA((4,)),
-                pltpu.SemaphoreType.DMA((n_dev,)),
-                pltpu.SemaphoreType.DMA((n_dev,)),
+                pltpu.VMEM(coarse.shape, f32),
+                pltpu.VMEM(fine.shape, f32),
+                pltpu.SemaphoreType.DMA((4 * PARTS,)),
+                pltpu.SemaphoreType.DMA((2,)),
+                pltpu.SemaphoreType.DMA((n_dev * PARTS,)),
+                pltpu.SemaphoreType.DMA((PARTS, n_dev)),
                 pltpu.SemaphoreType.DMA((groups,)),
                 pltpu.SemaphoreType.DMA((groups,)),
                 pltpu.SemaphoreType.DMA((groups,)),
@@ -310,7 +360,7 @@
             ),
         )(source_pick, pair_remote, pair_local, pair_count, spectra, jnp.asarray(coarse), jnp.asarray(fine))
         return (
-            jnp.transpose(group_corr, (1, 0, 2)),
+            group_corr,
             cross_corr.reshape(1, 1, groups, slots, LAGS),
         )
 

time: 25.7 us -> 23.2 us (0.903)
  Pallas kernels: 21.9 us -> 19.4 us
    pallas_call x1, Pallas kernels: 21.9 us -> 19.4 us  [on_device(): pl.pallas_call(functools.partial(kernel, groups, n_dev, slots, channels,...]
where the time goes in v2:
time: 23.2 us; the launch traced here: 23 us
  Pallas kernels  19.4 us (84%)
  local copies, waits for them, and re-layouts  2.28 us (10%)
  between operations  1.29 us (6%)
    pallas_call x1, Pallas kernels, on_device(): pl.pallas_call(functools.partial(kernel, groups, n_dev, slots, channels,...  19.4 us
    unnamed x4, local copies, waits for them, and re-layouts  2.28 us

profile of v2, /device:TPU:0, one launch (start us, length us, event | category | flops | bytes accessed | tf_op | source)
XLA Modules:
  0.0 23.0 jit_solution(5047400019734496161)
XLA Ops:
  1.3 19.4 %shard_map.86 = (f32[8,16,512]{2,1,0:T(8,128)}, f32[2,2,512]{2,1,0:T(2,128)}) custom-call(s32[1]{0:T(128)S(6)} %copy.11.pick_ref, s32[1,1,2,2]{3,2,1,0:T(2,128)} %remote_ref.1, s32[1,1,2,2]{3,2,1,0:T(2,128)} %local_ref.1, s32[1,1,2]{2,1,0:T(1,128)} %count_ref.1, f32[8,2,2,4096]{3,2,1,0:T(2,128)} %x_hbm.1, f32[2,64,128]{2,1,0:T(8,128)} %constant.4.clone.coarse_hbm, ...), custom_call_target="tpu_custom_call" | custom-call | tf_op jit(solution)/shard_map/pallas_call | solution.py:321
  20.7 0.0 copy-start
  20.7 1.7 %copy.12 = f32[8,16,512]{2,1,0:T(8,128)} copy(f32[8,16,512]{2,1,0:T(8,128)} %get-tuple-element.8) | data formatting | bytes 524288
  22.4 0.0 copy-done
  22.4 0.6 %copy.13 = f32[1,1,2,2,512]{4,3,2,1,0:T(2,128)} copy(f32[1,1,2,2,512]{4,3,2,1,0:T(2,128)S(1)} %bitcast.1) | data formatting | bytes 16384
Async XLA Ops:
  20.7 1.7 %copy-start = (f32[2,2,512]{2,1,0:T(2,128)S(1)}, f32[2,2,512]{2,1,0:T(2,128)}, u32[]{:S(2)}) copy-start(f32[2,2,512]{2,1,0:T(2,128)} %get-tuple-element.5) | copy-start | bytes 24580

commit v3 on v2

--- a/solution.py
+++ b/solution.py
@@ -18,6 +18,7 @@
 WIDE = F // CHUNKS
 LANES = 128
 PARTS = 2
+TABLE_CUTS = (6, 10, 14, 16)
 PART = F // PARTS
 
 
@@ -34,7 +35,7 @@
 
 def kernel(
     groups, n_dev, slots, channels, pair_rows,
-    pick_ref, remote_ref, local_ref, count_ref, x_hbm, coarse_hbm, fine_hbm,
+    pick_ref, remote_ref, local_ref, x_hbm, coarse_hbm, fine_hbm,
     group_out, cross_out,
     raw, white, mag, gathered, row_scratch, src_f32, cos_t, sin_t, xr, xi, pr, pi, acc,
     req_out, req_in, rows_out, rows_in,
@@ -169,8 +170,29 @@
             arrived(q, j)
             forward(q, j, flip_k)
 
+    coarse_rows = F // FINE
+
+    cuts = [coarse_rows * n // 16 for n in TABLE_CUTS]
+
+    def table_part(first, last):
+        if first == last:
+            return
+
+        @pl.loop(first, last)
+        def _(a):
+            ac, asin = coarse_ref[0, pl.ds(a, 1), :], coarse_ref[1, pl.ds(a, 1), :]
+            here = pl.ds(pl.multiple_of(a * FINE, FINE), FINE)
+            for l in range(LAGS // LANES):
+                cols = slice(l * LANES, (l + 1) * LANES)
+                bc, bs = fine_ref[0, :, cols], fine_ref[1, :, cols]
+                cos_t[here, cols] = (ac * bc - asin * bs).astype(jnp.bfloat16)
+                sin_t[here, cols] = (-(asin * bc + ac * bs)).astype(jnp.bfloat16)
+
     whiten(0)
     pick_source(0)
+    for copy in table_loads:
+        copy.wait()
+    table_part(0, cuts[0])
     pl.semaphore_wait(barrier, rows + 1 + groups - 1)
     send_own(0)
     for t in range(1, groups):
@@ -198,21 +220,6 @@
         copy = remote(rows_out.at[t], rows_in.at[g], row_send.at[t], row_recv.at[g], (h, d))
         copy.start()
         started.append(copy)
-
-    for copy in table_loads:
-        copy.wait()
-    coarse_rows = F // FINE
-
-    def table_part(first, last):
-        @pl.loop(first, last)
-        def _(a):
-            ac, asin = coarse_ref[0, pl.ds(a, 1), :], coarse_ref[1, pl.ds(a, 1), :]
-            here = pl.ds(pl.multiple_of(a * FINE, FINE), FINE)
-            for l in range(LAGS // LANES):
-                cols = slice(l * LANES, (l + 1) * LANES)
-                bc, bs = fine_ref[0, :, cols], fine_ref[1, :, cols]
-                cos_t[here, cols] = (ac * bc - asin * bs).astype(jnp.bfloat16)
-                sin_t[here, cols] = (-(asin * bc + ac * bs)).astype(jnp.bfloat16)
 
     def cross_chip(q, first):
         for half in range(2):
@@ -255,12 +262,14 @@
         )
         acc[...] = part if q == 0 else acc[...] + part
 
-    table_part(0, coarse_rows // 2)
+    table_part(cuts[0], cuts[1])
     pass_column(0)
-    table_part(coarse_rows // 2, coarse_rows)
+    table_part(cuts[1], cuts[2])
     for q in range(1, PARTS):
         pass_column(q)
+        table_part(cuts[2], cuts[3])
         pass_other(q - 1)
+    table_part(cuts[3], coarse_rows)
 
     if pair_rows:
         pr[...] = jnp.zeros_like(pr)
@@ -290,16 +299,12 @@
             pass_other(PARTS - 1)
         multiply(q)
 
-    scale = 0.5 * F ** (-0.5)
     for j in range(n_dev):
-        group_out[:, j, :] = acc[j * channels:(j + 1) * channels, :] * scale
+        group_out[:, j, :] = acc[j * channels:(j + 1) * channels, :]
     cross_out[g] = jnp.zeros((slots, LAGS), jnp.float32)
     for t in range(1, groups):
-        h = group_of(t)
-        for slot in range(slots):
-            row = n_dev * channels + (t - 1) * slots + slot
-            valid = jnp.where(slot < count_ref[0, 0, h], scale, 0.0)
-            cross_out[h, slot:slot + 1, :] = acc[row:row + 1, :] * valid
+        row = n_dev * channels + (t - 1) * slots
+        cross_out[group_of(t)] = acc[row:row + slots, :]
 
     for copy in started:
         copy.wait_send()
@@ -315,7 +320,7 @@
         pair_rows = -(-((groups - 1) * slots) // 16) * 16
         total = n_dev * channels + pair_rows
         smem = pl.BlockSpec(memory_space=pltpu.SMEM)
-        hbm = pl.BlockSpec(memory_space=pl.ANY)
+        hbm = pl.BlockSpec(memory_space=pltpu.HBM)
         vmem = pl.BlockSpec(memory_space=pltpu.VMEM)
         f32, bf16 = jnp.float32, jnp.bfloat16
         group_corr, cross_corr = pl.pallas_call(
@@ -324,7 +329,7 @@
                 jax.ShapeDtypeStruct((channels, n_dev, LAGS), f32),
                 jax.ShapeDtypeStruct((groups, slots, LAGS), f32),
             ),
-            in_specs=[smem, smem, smem, smem, hbm, hbm, hbm],
+            in_specs=[smem, smem, smem, hbm, hbm, hbm],
             out_specs=(vmem, vmem),
             scratch_shapes=[
                 pltpu.VMEM((4, channels, F), f32),
@@ -358,11 +363,26 @@
             compiler_params=pltpu.CompilerParams(
                 collective_id=0, has_side_effects=True, vmem_limit_bytes=56 << 20
             ),
-        )(source_pick, pair_remote, pair_local, pair_count, spectra, jnp.asarray(coarse), jnp.asarray(fine))
-        return (
-            group_corr,
-            cross_corr.reshape(1, 1, groups, slots, LAGS),
-        )
+        )(source_pick, pair_remote, pair_local, spectra, jnp.asarray(coarse), jnp.asarray(fine))
+        scale = 0.5 * F ** (-0.5)
+
+        def finish(count_ref, group_ref, cross_ref, group_out, cross_out):
+            group_out[...] = group_ref[...] * scale
+            for h in range(groups):
+                for slot in range(slots):
+                    valid = slot < count_ref[0, 0, h]
+                    cross_out[0, 0, h, slot:slot + 1, :] = jnp.where(valid, cross_ref[h, slot:slot + 1, :] * scale, 0.0)
+
+        group_corr, cross_corr = pl.pallas_call(
+            finish,
+            out_shape=(
+                jax.ShapeDtypeStruct((channels, n_dev, LAGS), f32),
+                jax.ShapeDtypeStruct((1, 1, groups, slots, LAGS), f32),
+            ),
+            in_specs=[smem, vmem, vmem],
+            out_specs=(vmem, vmem),
+        )(pair_count, group_corr, cross_corr)
+        return group_corr, cross_corr
 
     return jax.shard_map(
         on_device,

time: 23.2 us -> 21.2 us (0.914)
  local copies, waits for them, and re-layouts: 2.28 us -> 0 us
  Pallas kernels: 19.4 us -> 19.8 us
    unnamed x4 -> x0, local copies, waits for them, and re-layouts: 2.28 us -> none
    pallas_call x0 -> x1, Pallas kernels: none -> 1.69 us  [on_device(): pl.pallas_call(finish, out_shape=(jax.ShapeDtypeStruct((channels, n_dev,...]
    pallas_call x1, Pallas kernels: 19.4 us -> 18.1 us  [on_device(): pl.pallas_call(functools.partial(kernel, groups, n_dev, slots, channels,...]
where the time goes in v3:
time: 21.2 us; the launch traced here: 21 us
  Pallas kernels  19.8 us (93%)
  between operations  1.28 us (6%)
    pallas_call x1, Pallas kernels, on_device(): pl.pallas_call(functools.partial(kernel, groups, n_dev, slots, channels,...  18.1 us
    pallas_call x1, Pallas kernels, on_device(): pl.pallas_call(finish, out_shape=(jax.ShapeDtypeStruct((channels, n_dev,...  1.69 us

profile of v3, /device:TPU:0, one launch (start us, length us, event | category | flops | bytes accessed | tf_op | source)
XLA Modules:
  0.0 21.0 jit_solution(4185916532489868616)
XLA Ops:
  1.3 18.1 %shard_map.86 = (f32[8,16,512]{2,1,0:T(8,128)}, f32[2,2,512]{2,1,0:T(2,128)}) custom-call(s32[1]{0:T(128)S(6)} %copy.9.pick_ref, s32[1,1,2,2]{3,2,1,0:T(2,128)} %remote_ref.1, s32[1,1,2,2]{3,2,1,0:T(2,128)} %local_ref.1, f32[8,2,2,4096]{3,2,1,0:T(2,128)} %x_hbm.1, f32[2,64,128]{2,1,0:T(8,128)} %constant.4.clone.coarse_hbm, f32[2,64,512]{2,1,0:T(8,128)} %constant.5.clone.fine_hbm), custom_call_target="tpu_custom_call" | custom-call | tf_op jit(solution)/shard_map/pallas_call | solution.py:326
  19.4 1.7 %shard_map.87 = (f32[8,16,512]{2,1,0:T(8,128)}, f32[1,1,2,2,512]{4,3,2,1,0:T(2,128)}) custom-call(s32[1,1,2]{2,1,0:T(1,128)} %count_ref.1, f32[8,16,512]{2,1,0:T(8,128)} %get-tuple-element.4.group_ref, f32[2,2,512]{2,1,0:T(2,128)} %get-tuple-element.5.cross_ref), custom_call_target="tpu_custom_call" | custom-call | tf_op jit(solution)/shard_map/pallas_call | solution.py:376

commit v4 on v3

--- a/solution.py
+++ b/solution.py
@@ -17,7 +17,7 @@
 CHUNKS = 4
 WIDE = F // CHUNKS
 LANES = 128
-PARTS = 2
+PARTS = 1
 TABLE_CUTS = (6, 10, 14, 16)
 PART = F // PARTS
 
@@ -269,7 +269,11 @@
         pass_column(q)
         table_part(cuts[2], cuts[3])
         pass_other(q - 1)
-    table_part(cuts[3], coarse_rows)
+    if PARTS == 1:
+        table_part(cuts[2], coarse_rows)
+        pass_other(0)
+    else:
+        table_part(cuts[3], coarse_rows)
 
     if pair_rows:
         pr[...] = jnp.zeros_like(pr)

time: 21.2 us -> 21.1 us (level)
  no operation moved by 1% of the time
where the time goes in v4:
time: 21.1 us; the launch traced here: 20.9 us
  Pallas kernels  19.6 us (93%)
  between operations  1.28 us (6%)
    pallas_call x1, Pallas kernels, on_device(): pl.pallas_call(functools.partial(kernel, groups, n_dev, slots, channels,...  17.9 us
    pallas_call x1, Pallas kernels, on_device(): pl.pallas_call(finish, out_shape=(jax.ShapeDtypeStruct((channels, n_dev,...  1.69 us

profile of v4, /device:TPU:0, one launch (start us, length us, event | category | flops | bytes accessed | tf_op | source)
XLA Modules:
  0.0 20.9 jit_solution(6253114799894253831)
XLA Ops:
  1.3 17.9 %shard_map.86 = (f32[8,16,512]{2,1,0:T(8,128)}, f32[2,2,512]{2,1,0:T(2,128)}) custom-call(s32[1]{0:T(128)S(6)} %copy.9.pick_ref, s32[1,1,2,2]{3,2,1,0:T(2,128)} %remote_ref.1, s32[1,1,2,2]{3,2,1,0:T(2,128)} %local_ref.1, f32[8,2,2,4096]{3,2,1,0:T(2,128)} %x_hbm.1, f32[2,64,128]{2,1,0:T(8,128)} %constant.4.clone.coarse_hbm, f32[2,64,512]{2,1,0:T(8,128)} %constant.5.clone.fine_hbm), custom_call_target="tpu_custom_call" | custom-call | tf_op jit(solution)/shard_map/pallas_call | solution.py:330
  19.2 1.7 %shard_map.87 = (f32[8,16,512]{2,1,0:T(8,128)}, f32[1,1,2,2,512]{4,3,2,1,0:T(2,128)}) custom-call(s32[1,1,2]{2,1,0:T(1,128)} %count_ref.1, f32[8,16,512]{2,1,0:T(8,128)} %get-tuple-element.4.group_ref, f32[2,2,512]{2,1,0:T(2,128)} %get-tuple-element.5.cross_ref), custom_call_target="tpu_custom_call" | custom-call | tf_op jit(solution)/shard_map/pallas_call | solution.py:380
